TPU v7x, 128 devices: a whole 4x4x4 slice. The times are simulated.
128 devices in a mesh: ctx: 16 (over x_lo, z, core), mp: 4 (over y), rep: 2 (over x_hi).
Axes of the slice: x: 4 (x_hi: 2, x_lo: 2; x = x_hi * 2 + x_lo), y: 4, z: 4, core: 2. Of those that a mesh axis runs over, the one named last changes fastest.
Arguments:
- token_pages: bfloat16 [128, 128, 2048], P('ctx'), may hold values from -13 to 13
- page_table: int32 [128], P('ctx'), may hold values from 0 to 7, as said below
- live_flags: int32 [128], P('ctx'), may hold values from 0 to 1, as said below
- lengths: int32 [32], replicated, may hold values from 1 to 1024, as said below
- decay_floor: float32 [2048], P(('mp', 'rep')), may hold values from 0.85 to 0.9998
- mixer_gain: float32 [2048], replicated, may hold values from 0.5 to 1.5
- feed_gain: float32 [2048], replicated, may hold values from 0.5 to 1.5
- trainer_mixer_in: float32 [3, 2048, 2048], P(None, ('ctx', 'mp')), may hold values from -0.125 to 0.125
- trainer_mixer_out: float32 [2048, 2048], P(None, ('ctx', 'mp')), may hold values from -0.125 to 0.125
- trainer_gate_up: float32 [2, 2048, 5632], P(None, ('ctx', 'mp')), may hold values from -0.125 to 0.125
- trainer_down: float32 [5632, 2048], P(None, ('ctx', 'mp')), may hold values from -0.078125 to 0.078125
Outputs:
- layer_output: bfloat16 [16384, 2048], P(('ctx', 'rep'), 'mp')
Inputs may be any that keep to these rules, and one draw needn't show every extreme that they name: `page_table`: within each device's block of 8 entries every value 0 to 7 appears once. `live_flags`: in each device's block of 8 flags at least half (rounded down, and never fewer than one) are ones, and some device's block is all ones. The lengths sum to 128 times the number of ones in live_flags; one prompt has exactly 1024 tokens.
All inputs are finite; a program needn't handle non-finite values.
Results may differ from a plain program's by a relative error of at most 0.015.
Values may be sent and summed in bfloat16 or wider, within the bound.
A program may use at most 192 MiB of HBM per device.

v0:
```python
import jax
import jax.numpy as jnp
from jax import lax
from jax.sharding import PartitionSpec as P

D = 2048
HEADS = 16
norm_eps = 1e-05


def prefix(value, axis, join, neutral):
    count, mine = (lax.axis_size(axis), lax.axis_index(axis))
    pieces = lax.all_gather(value, axis)
    total = jnp.full_like(value, 0) + jnp.asarray(neutral, value.dtype)

    def prefix_step(position, total):
        longer = join(total, pieces[position])
        return jnp.where(position < mine, longer, total)

    return lax.fori_loop(0, count - 1, prefix_step, total)


def entering_2(shard, axis, combine, identity):
    peers, position = (lax.axis_size(axis), lax.axis_index(axis))
    everything = jax.tree.map(
        lambda part, kind: lax.all_gather(part.astype(kind), axis),
        shard,
        (jnp.bfloat16, jnp.bfloat16),
    )
    start = jax.tree.map(
        lambda part, zero: jnp.broadcast_to(jnp.asarray(zero, part.dtype), part.shape),
        shard,
        identity,
    )

    def entering_step(k, before):
        reached = k < position
        new = combine(
            before, jax.tree.map(lambda part, own: part[k].astype(own.dtype), everything, shard)
        )
        return jax.tree.map(lambda a, b: jnp.where(reached, a, b), new, before)

    return lax.fori_loop(0, peers, entering_step, start)


def rms_scale(values_in, gain):
    mean_sq = jnp.mean(values_in * values_in, axis=-1, keepdims=True)
    return values_in * lax.rsqrt(mean_sq + norm_eps) * gain


def block_recurrence(queries, keys_in, values_in, log_decay, reset_count, state_init, count_init):
    highest = lax.Precision.HIGHEST

    def advance(carried_in, block_data):
        state, count_before = carried_in
        q_block, k_block, v_block, decay_block, count_block = block_data
        cumulative = jnp.cumsum(decay_block, axis=0)
        q_scaled = q_block * jnp.exp(cumulative)
        k_scaled = k_block * jnp.exp(-cumulative)
        scores = jnp.einsum("thd,shd->hts", q_scaled, k_scaled, precision=highest)
        positions = jnp.arange(count_block.shape[0])
        allowed = (positions[:, None] >= positions[None, :]) & (
            count_block[:, None] == count_block[None, :]
        )
        scores = jnp.where(allowed[None], scores, 0.0)
        outputs = jnp.einsum("hts,shd->thd", scores, v_block, precision=highest)
        from_state = jnp.einsum("thd,hde->the", q_scaled, state, precision=highest)
        outputs = outputs + jnp.where((count_block == count_before)[:, None, None], from_state, 0.0)
        last_count = count_block[-1]
        final_cum = cumulative[-1]
        weight_keys = (
            k_block
            * jnp.exp(final_cum[None] - cumulative)
            * (count_block == last_count).astype(k_block.dtype)[:, None, None]
        )
        retained = jnp.where(
            last_count == count_before, jnp.exp(final_cum)[:, :, None] * state, 0.0
        )
        state_next = retained + jnp.einsum("thd,the->hde", weight_keys, v_block, precision=highest)
        return ((state_next, last_count), outputs)

    final_carry, outputs_all = lax.scan(
        advance, (state_init, count_init), (queries, keys_in, values_in, log_decay, reset_count)
    )
    return (outputs_all, final_carry[0])


def compose_states(earlier, later):
    return (earlier[0] * later[0], later[0][:, :, None] * earlier[1] + later[1])


def add_counts(earlier, later):
    return earlier + later


def shards(
    token_pages,
    page_table,
    live_flags,
    lengths,
    decay_floor,
    mixer_gain,
    feed_gain,
    trainer_mixer_in,
    trainer_mixer_out,
    trainer_gate_up,
    trainer_down,
):
    mp_count = lax.axis_size("mp")
    rep_count = lax.axis_size("rep")
    mp_index = lax.axis_index("mp")
    rep_index = lax.axis_index("rep")
    width_local = trainer_mixer_in.shape[1]
    model_width = trainer_mixer_in.shape[2]
    head_cols = decay_floor.shape[0]
    head_dim = D // HEADS
    local_heads = head_cols // head_dim
    hidden_block = trainer_gate_up.shape[2] // mp_count
    mixer_in = lax.dynamic_index_in_dim(
        trainer_mixer_in.reshape(3, width_local, mp_count, rep_count, head_cols),
        rep_index,
        3,
        keepdims=False,
    )
    mixer_in = jnp.transpose(mixer_in, (1, 2, 0, 3)).reshape(width_local, mp_count, 3 * head_cols)
    mixer_out = lax.dynamic_index_in_dim(
        trainer_mixer_out.reshape(mp_count, rep_count, head_cols, width_local),
        rep_index,
        1,
        keepdims=False,
    )
    mixer_out = jnp.transpose(mixer_out, (2, 0, 1))
    gate_up = trainer_gate_up.reshape(2, width_local, mp_count, hidden_block)
    down_rows = trainer_down.reshape(mp_count, hidden_block, width_local)
    gate_up = jnp.transpose(gate_up, (1, 2, 0, 3)).reshape(width_local, mp_count, 2 * hidden_block)
    down_rows = jnp.transpose(down_rows, (2, 0, 1))
    packed = jnp.concatenate([mixer_in, mixer_out, gate_up, down_rows], axis=2).astype(jnp.bfloat16)
    arrived = lax.all_to_all(packed, "mp", split_axis=1, concat_axis=0, tiled=True)
    arrived = arrived.reshape(mp_count * width_local, packed.shape[2])
    served = lax.all_gather(arrived, "ctx", axis=0, tiled=True)
    w_mixer = served[:, : 3 * head_cols]
    w_output_t = served[:, 3 * head_cols : 4 * head_cols]
    feed_weights = served[:, 4 * head_cols :].reshape(model_width, 3, hidden_block)
    pages_local = token_pages.shape[0]
    page_len = token_pages.shape[1]
    tok_count = pages_local * page_len
    ordered = jnp.take(token_pages, page_table, axis=0).reshape(tok_count, model_width)
    live_tokens = jnp.repeat(live_flags, page_len)
    page_live = live_flags * page_len
    live_total = jnp.sum(page_live)
    stream_base = prefix(live_total, "ctx", add_counts, jnp.zeros((), jnp.int32))
    page_start = stream_base + jnp.cumsum(page_live) - page_live
    positions = (page_start[:, None] + jnp.arange(page_len, dtype=jnp.int32)[None, :]).reshape(
        tok_count
    )
    starts = jnp.cumsum(lengths) - lengths
    resets = (live_tokens == 1) & jnp.any(positions[:, None] == starts[None, :], axis=1)
    reset_count = jnp.cumsum(resets.astype(jnp.int32))
    live_float = live_tokens.astype(jnp.float32)[:, None]
    normed = rms_scale(ordered.astype(jnp.float32), mixer_gain).astype(jnp.bfloat16)
    projected = jnp.dot(normed, w_mixer, preferred_element_type=jnp.float32).reshape(
        tok_count, 3, head_cols
    )
    queries = jax.nn.silu(projected[:, 0])
    forget = decay_floor + (1.0 - decay_floor) * jax.nn.sigmoid(projected[:, 1])
    log_decay = jnp.log(forget) * live_float
    keys_in = (1.0 - forget) * live_float
    values_in = projected[:, 2]
    shape_blocks = (pages_local, page_len, local_heads, head_dim)
    local_out, local_state = block_recurrence(
        queries.reshape(shape_blocks),
        keys_in.reshape(shape_blocks),
        values_in.reshape(shape_blocks),
        log_decay.reshape(shape_blocks),
        reset_count.reshape(pages_local, page_len),
        jnp.zeros((local_heads, head_dim, head_dim), jnp.float32),
        jnp.zeros((), jnp.int32),
    )
    device_decay = jnp.where(
        reset_count[-1] == 0, jnp.exp(jnp.sum(log_decay, axis=0)), 0.0
    ).reshape(local_heads, head_dim)
    identity = (
        jnp.ones((local_heads, head_dim), jnp.float32),
        jnp.zeros((local_heads, head_dim, head_dim), jnp.float32),
    )
    entering = entering_2((device_decay, local_state), "ctx", compose_states, identity)[1]
    cum_device = jnp.cumsum(log_decay, axis=0).reshape(tok_count, local_heads, head_dim)
    scaled_queries = queries.reshape(tok_count, local_heads, head_dim) * jnp.exp(cum_device)
    correction = jnp.einsum(
        "thd,hde->the", scaled_queries, entering, precision=lax.Precision.HIGHEST
    )
    mixed = local_out.reshape(tok_count, local_heads, head_dim) + jnp.where(
        (reset_count == 0)[:, None, None], correction, 0.0
    )
    head_normed = (
        (mixed * lax.rsqrt(jnp.mean(mixed * mixed, axis=-1, keepdims=True) + norm_eps))
        .reshape(tok_count, head_cols)
        .astype(jnp.bfloat16)
    )
    half_rows = tok_count // rep_count
    col_block = model_width // mp_count
    attn_term = lax.dot_general(
        head_normed, w_output_t, (((1,), (1,)), ((), ())), preferred_element_type=jnp.float32
    )
    attn_all = lax.psum(attn_term.astype(jnp.bfloat16), ("mp", "rep")).astype(jnp.float32)
    residual = lax.dynamic_slice_in_dim(ordered, rep_index * half_rows, half_rows, 0).astype(
        jnp.float32
    ) + lax.dynamic_slice_in_dim(attn_all, rep_index * half_rows, half_rows, 0)
    feed_in = rms_scale(residual, feed_gain).astype(jnp.bfloat16)
    gated = jnp.einsum(
        "td,dcf->tcf", feed_in, feed_weights[:, :2], preferred_element_type=jnp.float32
    )
    hidden = (jax.nn.silu(gated[:, 0]) * gated[:, 1]).astype(jnp.bfloat16)
    down_term = lax.dot_general(
        hidden, feed_weights[:, 2], (((1,), (1,)), ((), ())), preferred_element_type=jnp.float32
    )
    summed = lax.psum_scatter(
        down_term.astype(jnp.bfloat16), "mp", scatter_dimension=1, tiled=True
    ).astype(jnp.float32)
    summed = summed + lax.dynamic_slice_in_dim(residual, mp_index * col_block, col_block, 1)
    live_half = lax.dynamic_slice_in_dim(live_tokens, rep_index * half_rows, half_rows, 0)
    return jnp.where(live_half[:, None] == 1, summed, 0.0).astype(jnp.bfloat16)


def solution(mesh):
    in_specs = (
        P("ctx", None, None),
        P("ctx"),
        P("ctx"),
        P(),
        P(("mp", "rep")),
        P(),
        P(),
        P(None, ("ctx", "mp"), None),
        P(None, ("ctx", "mp")),
        P(None, ("ctx", "mp"), None),
        P(None, ("ctx", "mp")),
    )
    out_specs = P(("ctx", "rep"), "mp")
    return jax.shard_map(shards, mesh=mesh, in_specs=in_specs, out_specs=out_specs, check_vma=False)
```

profile of v0, /device:TPU:1, one launch (start us, length us, event | category | flops | bytes accessed | tf_op | source)
XLA Modules:
  0.0 575.1 jit_solution(12584117254873081062)
XLA Ops:
  12.5 22.0 %all_to_all.15 = bf16[32,4,5248]{2,0,1:T(8,128)(2,1)} all-to-all(bf16[32,4,5248]{2,0,1:T(8,128)(2,1)S(1)} %pad_maximum_fusion), channel_id=1, replica_groups=mesh['ctx'=16,'mp'=4,'rep'=2] {'mp'}, dimensions={1} | all-to-all | bytes 2686976 | tf_op jit(solution)/shard_map/all_to_all | solution.py:138
  37.6 13.0 %all-reduce = s32[16]{0:T(128)S(1)} all-reduce(s32[16]{0:T(128)S(1)} %dynamic-update-slice), channel_id=1, replica_groups=mesh['ctx'=16,'mp'=4,'rep'=2] {'ctx'}, use_global_device_ids=true, to_apply=%add | all-reduce | flops 16 | bytes 128
  50.7 18.5 %while.42 = (s32[]{:T(128)}, s32[]{:T(128)}, s32[]{:T(128)}, s32[16]{0:T(128)S(1)}, s32[]{:T(128)}) while((s32[]{:T(128)}, s32[]{:T(128)}, s32[]{:T(128)}, s32[16]{0:T(128)S(1)}, s32[]{:T(128)}) %tuple.96), condition=%wide.region_3.4_spmd, body=%wide.region_2.3_spmd.sunk | while | flops 5 | bytes 107 | solution.py:20
  69.8 5.1 gather_fusion
  82.0 68.7 %all-gather.4.cloned.1.call-done = bf16[2048,5248]{1,0:T(8,128)(2,1)} async-done(((bf16[128,5248]{1,0:T(8,128)(2,1)}), bf16[2048,5248]{1,0:T(8,128)(2,1)}) %all-gather.4.cloned.1.call-update) | async-done | bytes 21495824 | tf_op jit(solution)/shard_map/all_gather | solution.py:140
  155.8 6.2 %fusion.62 = f32[1024,3,256]{2,0,1:T(8,128)S(1)} fusion(bf16[1024,2048,1]{1,0,2:T(8,128)(2,1)} %bitcast.193, bf16[3,256,2048]{2,1,0:T(8,128)(2,1)} %bitcast.197), kind=kOutput, calls=%fused_computation.127 | convolution fusion | flops 3221225472 | bytes 10485760 | tf_op jit(solution)/shard_map/dot_general | solution.py:161
  177.1 95.7 %while.43 = (s32[]{:T(128)}, f32[2,128,128]{2,1,0:T(8,128)S(1)}, s32[]{:T(128)}, f32[8,128,2,128]{1,0,3,2:T(8,128)}, s32[8,128]{1,0:T(8,128)S(1)}, /*index=5*/f3...) while((s32[]{:T(128)}, f32[2,128,128]{2,1,0:T(8,128)S(1)}, ...), condition=%wide.region_11.12_spmd.clone, body=%wide.region_9.11_spmd.clone.sunk | while | flops 205996416 | bytes 3712938 | solution.py:82
  182.7 4.8 dynamic_update_slice.6
  194.7 4.8 dynamic_update_slice.6
  206.6 4.8 dynamic_update_slice.6
  218.6 4.8 dynamic_update_slice.6
  230.6 4.8 dynamic_update_slice.6
  242.5 4.8 dynamic_update_slice.6
  254.5 4.8 dynamic_update_slice.6
  266.5 4.8 dynamic_update_slice.6
  282.2 18.9 %all_gather.22 = bf16[16,2,128]{2,1,0:T(2,128)(2,1)S(1)} all-gather(bf16[1,2,128]{2,1,0:T(2,128)(2,1)S(1)} %fusion.52), channel_id=1, replica_groups=mesh['ctx'=16,'mp'=4,'rep'=2] {'ctx'}, dimensions={0}, use_global_device_ids=true | all-gather | bytes 8704 | tf_op jit(solution)/shard_map/all_gather | solution.py:26
  301.1 6.1 %all-gather.6.cloned.1.call-done = bf16[32,128,128]{2,1,0:T(8,128)(2,1)} async-done(((bf16[2,128,128]{2,1,0:T(8,128)(2,1)}), bf16[32,128,128]{2,1,0:T(8,128)(2,1)}) %all-gather.6.cloned.1.call-update) | async-done | bytes 1048592 | tf_op jit(solution)/shard_map/all_gather | solution.py:26
  307.2 16.2 %while.44 = (s32[]{:T(128)}, f32[2,128,128]{2,1,0:T(8,128)S(1)}, s32[]{:T(128)}, bf16[16,2,128]{2,1,0:T(2,128)(2,1)S(1)}, bf16[16,2,128,128]{3,2,1,0:T(8,128)(2,1)}, /*index=5*/s32[]{:T(128)}, s32[]{:T(128)}) while((s32[]{:T(128)}, f32[2,128,128]{2,1,0:T(8,128)S(1)}, s32[]{:T(128)}, bf16[16,2,128]{2,1,0:T(2,128)(2,1)S(1)}, ...), condition=%wide.region_14.15_spmd.clone, body=%wide.region_13.14_spmd.clone.sunk | while | flops 164100 | bytes 330345 | solution.py:43
  331.2 14.2 %slice.81 = bf16[2048,4224]{1,0:T(8,128)(2,1)} slice(bf16[2048,5248]{1,0:T(8,128)(2,1)} %all-gather.4.cloned.1.call-done), slice={[0:2048], [1024:5248]} | slice | bytes 34603008 | tf_op jit(solution)/shard_map/slice | solution.py:143
  345.4 22.6 %copy.114 = bf16[2048,4224]{0,1:T(8,128)(2,1)} copy(bf16[2048,4224]{1,0:T(8,128)(2,1)} %slice.81) | data formatting | bytes 34603008 | tf_op jit(solution)/shard_map/slice | solution.py:143
  368.0 147.3 %all-reduce.3.cloned.1.call-done = bf16[1024,2048]{1,0:T(8,128)(2,1)} async-done(((bf16[1024,2048]{1,0:T(8,128)(2,1)}), bf16[1024,2048]{1,0:T(8,128)(2,1)}) %all-reduce.3.cloned.1.call-update) | async-done | bytes 4194320 | tf_op jit(solution)/shard_map/psum | solution.py:205
  518.5 11.2 %fusion.19 = f32[512,2,1408]{2,0,1:T(8,128)S(1)} fusion(bf16[2048,3,1408]{0,2,1:T(8,128)(2,1)} %bitcast.190, f32[512,2048]{1,0:T(8,128)S(1)} %get-tuple-element.362, f32[2048]{0:T(1024)S(1)} %copy-done.9, f32[512]{0:T(512)S(1)} %add_rsqrt_fusion.2), kind=kOutput, calls=%fused_computation.36 | convolution fusion | flops 5908725760 | bytes 21506048 | tf_op jit(solution)/shard_map/td,dcf->tcf/dot_general | solution.py:210
  529.7 7.3 %fusion.25 = bf16[512,2048]{1,0:T(8,128)(2,1)} fusion(bf16[2048,3,1408]{0,2,1:T(8,128)(2,1)} %bitcast.191, f32[512,2,1408]{2,0,1:T(8,128)S(1)} %fusion.19), kind=kOutput, calls=%fused_computation.51 | convolution fusion | flops 2958163968 | bytes 13631488 | tf_op jit(solution)/shard_map/dot_general | solution.py:214
  537.2 29.1 %reduce-scatter.2.cloned.1.call-done = bf16[512,512]{1,0:T(8,128)(2,1)} async-done(((bf16[512,2048]{1,0:T(8,128)(2,1)}), bf16[512,512]{1,0:T(8,128)(2,1)}) %reduce-scatter.2.cloned.1.call-update) | async-done | bytes 524304 | tf_op jit(solution)/shard_map/reduce_scatter | solution.py:217
  (263 shorter events, 130.3 us)
Async XLA Ops:
  6.5 3.1 copy-start.3
  6.5 144.2 %all-gather.4.cloned.1.call-start = ((), (), s32[]{:S(2)}) async-start(), calls=%async_computation.2 | async-start | bytes 22839296 | tf_op jit(solution)/shard_map/all_gather | solution.py:140
  11.1 23.5 %copy-start.6 = (s32[8]{0:T(128)S(1)}, s32[8]{0:T(128)}, u32[]{:S(2)}) copy-start(s32[8]{0:T(128)} %param.19) | copy-start | bytes 100
  11.1 23.5 %copy-start.8 = (s32[8]{0:T(128)S(1)}, s32[8]{0:T(128)}, u32[]{:S(2)}) copy-start(s32[8]{0:T(128)} %param.18) | copy-start | bytes 100
  11.2 24.3 %copy-start.7 = (s32[32]{0:T(128)S(1)}, s32[32]{0:T(128)}, u32[]{:S(2)}) copy-start(s32[32]{0:T(128)} %param.20) | copy-start | bytes 388
  11.2 24.6 %copy-start.10 = (u32[128]{0:T(128)S(1)}, u32[128]{0:T(128)}, u32[]{:S(2)}) copy-start(u32[128]{0:T(128)} %constant.161) | copy-start | bytes 1540
  34.5 272.6 %all-gather.6.cloned.1.call-start = ((), (), s32[]{:S(2)}) async-start(), calls=%async_computation.5 | async-start | bytes 1114112 | tf_op jit(solution)/shard_map/all_gather | solution.py:26
  69.8 5.2 copy-start.4
  74.9 3.8 copy-start
  74.9 3.8 copy-start.5
  162.1 1.7 copy-start.2
  273.5 241.7 %all-reduce.3.cloned.1.call-start = ((), (), s32[]{:S(2)}) async-start(), calls=%async_computation.3 | async-start | bytes 8388608 | tf_op jit(solution)/shard_map/psum | solution.py:205
  331.0 235.3 %reduce-scatter.2.cloned.1.call-start = ((), (), s32[]{:S(2)}) async-start(), calls=%async_computation.4 | async-start | bytes 2621440 | tf_op jit(solution)/shard_map/reduce_scatter | solution.py:217
  515.3 3.2 copy-start.9
  518.5 11.2 %copy-start.1 = (f32[512,2048]{1,0:T(8,128)}, f32[512,2048]{1,0:T(8,128)S(1)}, u32[]{:S(2)}) copy-start(f32[512,2048]{1,0:T(8,128)S(1)} %get-tuple-element.362) | copy-start | bytes 12582916
Sparse Core Ops, SparseCore 0:
  34.7 116.0 all-gather.3
  273.7 33.4 all-gather.5
  331.1 184.1 all-reduce.2
  537.2 29.0 reduce-scatter.1
where the time goes:
time: 578 us; the launch traced here: 575 us
  waiting for transfers between devices  251 us (43%)
  local copies, waits for them, and re-layouts  127 us (22%)
  other arithmetic  65.4 us (11%)
  blocking collectives  54 us (9%)
  matrix products  42.7 us (7%)
  loops' own time  20.7 us (4%)
  between operations  14.2 us (2%)
    psum x1, waiting for transfers between devices, shards(): lax.psum(attn_term.astype(jnp.bfloat16), ('mp', 'rep')).astype(jnp.float32)  147 us
    all_gather x1, waiting for transfers between devices, shards(): served = lax.all_gather(arrived, 'ctx', axis=0, tiled=True)  68.7 us
    dynamic_update_slice x16, local copies, waits for them, and re-layouts, block_recurrence(): lax.scan(advance, (state_init, count_init), (queries, keys_in, values_in,...  38.8 us
    slice x2, local copies, waits for them, and re-layouts, shards(): served[:, 4 * head_cols:].reshape(model_width, 3, hidden_block)  36.8 us
    reduce_scatter x1, waiting for transfers between devices, shards(): lax.psum_scatter(down_term.astype(jnp.bfloat16), 'mp', scatter_dimension=...  29.1 us
    all_to_all x1, blocking collectives, shards(): lax.all_to_all(packed, 'mp', split_axis=1, concat_axis=0, tiled=True)  22 us
    all_gather x1, blocking collectives, entering_2(): lax.all_gather(part.astype(kind), axis)  18.9 us
    select_n x16, other arithmetic, entering_step(): return jax.tree.map(lambda a, b: jnp.where(reached, a, b), new, before)  15.5 us
  transfers between devices with their start and end apart: 4, of which 4 were waited for; matrix products, arithmetic and copies ran while one was open for 12% of the time, Pallas kernels for 0%

commit v1 on v0

--- a/solution.py
+++ b/solution.py
@@ -137,7 +137,9 @@
     packed = jnp.concatenate([mixer_in, mixer_out, gate_up, down_rows], axis=2).astype(jnp.bfloat16)
     arrived = lax.all_to_all(packed, "mp", split_axis=1, concat_axis=0, tiled=True)
     arrived = arrived.reshape(mp_count * width_local, packed.shape[2])
-    served = lax.all_gather(arrived, "ctx", axis=0, tiled=True)
+    served = jnp.concatenate(
+        lax.all_to_all(jnp.stack([arrived] * lax.axis_size("ctx")), "ctx", 0, 0), axis=0
+    )
     w_mixer = served[:, : 3 * head_cols]
     w_output_t = served[:, 3 * head_cols : 4 * head_cols]
     feed_weights = served[:, 4 * head_cols :].reshape(model_width, 3, hidden_block)

time: 578 us -> 849 us (1.47)
  blocking collectives: 54 us -> 371 us
  waiting for transfers between devices: 251 us -> 204 us
    unnamed x1, blocking collectives: 13 us -> 332 us
    all_gather x1 -> x0, waiting for transfers between devices: 68.7 us -> none  [shards(): served = lax.all_gather(arrived, 'ctx', axis=0, tiled=True)]
    psum x1, waiting for transfers between devices: 147 us -> 169 us  [shards(): lax.psum(attn_term.astype(jnp.bfloat16), ('mp', 'rep')).astype(jnp.float32)]
    slice x2 -> x1, local copies, waits for them, and re-layouts: 36.8 us -> 14.8 us  [shards(): served[:, 4 * head_cols:].reshape(model_width, 3, hidden_block)]
    reshape x0 -> x1, local copies, waits for them, and re-layouts: none -> 10.8 us  [shards(): jnp.concatenate(lax.all_to_all(jnp.stack([arrived] * lax.axis_size('ctx')...]
    another operation x8 -> x10, local copies, waits for them, and re-layouts: 0.85 us -> 9.51 us  [the longest x2 8.67 us: shards(): jnp.stack([arrived] * lax.axis_size('ctx'))]
  transfers between devices with their start and end apart: 4 -> 4, of which waited for: 4 -> 3; matrix products, arithmetic and copies ran while one was open for 12% -> 6% of each run, Pallas kernels for 0% -> 0%
where the time goes in v1:
time: 849 us; the launch traced here: 846 us
  blocking collectives  371 us (44%)
  waiting for transfers between devices  204 us (24%)
  local copies, waits for them, and re-layouts  123 us (14%)
  other arithmetic  65.2 us (8%)
  matrix products  39.9 us (5%)
  loops' own time  20.3 us (2%)
  between operations  14.3 us (2%)
  starting transfers between devices  8.61 us (1%)
    unnamed x1, blocking collectives  332 us
    psum x1, waiting for transfers between devices, shards(): lax.psum(attn_term.astype(jnp.bfloat16), ('mp', 'rep')).astype(jnp.float32)  169 us
    dynamic_update_slice x16, local copies, waits for them, and re-layouts, block_recurrence(): lax.scan(advance, (state_init, count_init), (queries, keys_in, values_in,...  38.7 us
    reduce_scatter x1, waiting for transfers between devices, shards(): lax.psum_scatter(down_term.astype(jnp.bfloat16), 'mp', scatter_dimension=...  29.1 us
    all_to_all x1, blocking collectives, shards(): lax.all_to_all(packed, 'mp', split_axis=1, concat_axis=0, tiled=True)  21.9 us
    all_gather x1, blocking collectives, entering_2(): lax.all_gather(part.astype(kind), axis)  17.3 us
  transfers between devices with their start and end apart: 4, of which 3 were waited for; matrix products, arithmetic and copies ran while one was open for 6% of the time, Pallas kernels for 0%

profile of v1, /device:TPU:1, one launch (start us, length us, event | category | flops | bytes accessed | tf_op | source)
XLA Modules:
  0.0 846.4 jit_solution(3530348017346799924)
XLA Ops:
  12.4 21.9 %all_to_all.20 = bf16[32,4,5248]{2,0,1:T(8,128)(2,1)S(1)} all-to-all(bf16[32,4,5248]{2,0,1:T(8,128)(2,1)S(1)} %pad_maximum_fusion), channel_id=1, replica_groups=mesh['ctx'=16,'mp'=4,'rep'=2] {'mp'}, dimensions={1} | all-to-all | bytes 2686976 | tf_op jit(solution)/shard_map/all_to_all | solution.py:138
  35.4 7.6 stack.3
  43.0 8.5 %all-to-all-start.1 = ((bf16[16,128,5248]{1,2,0:T(8,128)(2,1)}), bf16[16,128,5248]{1,2,0:T(8,128)(2,1)}, u32[]{:S(2)}, u32[]{:S(2)}) async-start(bf16[16,128,5248]{1,2,0:T(8,128)(2,1)} %stack.3), calls=%async_computation.1 | async-start | bytes 42991616 | tf_op jit(solution)/shard_map/all_to_all | solution.py:141
  54.7 331.8 %all-reduce = s32[16]{0:T(128)S(1)} all-reduce(s32[16]{0:T(128)S(1)} %dynamic-update-slice), channel_id=1, replica_groups=mesh['ctx'=16,'mp'=4,'rep'=2] {'ctx'}, use_global_device_ids=true, to_apply=%add | all-reduce | flops 16 | bytes 128
  386.5 19.3 %while.42 = (s32[]{:T(128)}, s32[]{:T(128)}, s32[]{:T(128)}, s32[16]{0:T(128)S(1)}, s32[]{:T(128)}) while((s32[]{:T(128)}, s32[]{:T(128)}, s32[]{:T(128)}, s32[16]{0:T(128)S(1)}, s32[]{:T(128)}) %tuple.96), condition=%wide.region_3.4_spmd, body=%wide.region_2.3_spmd.sunk | while | flops 5 | bytes 107 | solution.py:20
  406.5 5.0 gather_fusion
  418.6 10.8 %copy_bitcast_fusion.3 = bf16[2048,5248]{0,1:T(8,128)(2,1)S(1)} fusion(bf16[16,128,5248]{1,2,0:T(8,128)(2,1)} %all-to-all-done.1), kind=kLoop, calls=%fused_computation.36 | loop fusion | bytes 42991616 | tf_op jit(solution)/shard_map/reshape | solution.py:140
  429.8 4.9 copy-done.4
  452.2 94.8 %while.43 = (s32[]{:T(128)}, f32[2,128,128]{2,1,0:T(8,128)S(1)}, s32[]{:T(128)}, f32[8,128,2,128]{1,0,3,2:T(8,128)}, s32[8,128]{1,0:T(8,128)S(1)}, /*index=5*/f3...) while((s32[]{:T(128)}, f32[2,128,128]{2,1,0:T(8,128)S(1)}, ...), condition=%wide.region_11.12_spmd.clone, body=%wide.region_9.11_spmd.clone.sunk | while | flops 205996416 | bytes 3712938 | solution.py:82
  457.7 4.7 dynamic_update_slice.6
  469.5 4.7 dynamic_update_slice.6
  481.4 4.7 dynamic_update_slice.6
  493.2 4.7 dynamic_update_slice.6
  505.1 4.7 dynamic_update_slice.6
  516.9 4.7 dynamic_update_slice.6
  528.7 4.7 dynamic_update_slice.6
  556.0 17.3 %all_gather.18 = bf16[16,2,128]{2,1,0:T(2,128)(2,1)S(1)} all-gather(bf16[1,2,128]{2,1,0:T(2,128)(2,1)S(1)} %fusion.52), channel_id=1, replica_groups=mesh['ctx'=16,'mp'=4,'rep'=2] {'ctx'}, dimensions={0}, use_global_device_ids=true | all-gather | bytes 8704 | tf_op jit(solution)/shard_map/all_gather | solution.py:26
  573.3 5.1 all-gather.3.cloned.1.call-done
  578.5 16.2 %while.44 = (s32[]{:T(128)}, f32[2,128,128]{2,1,0:T(8,128)S(1)}, s32[]{:T(128)}, bf16[16,2,128]{2,1,0:T(2,128)(2,1)S(1)}, bf16[16,2,128,128]{3,2,1,0:T(8,128)(2,1)}, /*index=5*/s32[]{:T(128)}, s32[]{:T(128)}) while((s32[]{:T(128)}, f32[2,128,128]{2,1,0:T(8,128)S(1)}, s32[]{:T(128)}, bf16[16,2,128]{2,1,0:T(2,128)(2,1)S(1)}, ...), condition=%wide.region_14.15_spmd.clone, body=%wide.region_13.14_spmd.clone.sunk | while | flops 164100 | bytes 330345 | solution.py:43
  602.4 14.8 %slice.81 = bf16[2048,4224]{0,1:T(8,128)(2,1)} slice(bf16[2048,5248]{0,1:T(8,128)(2,1)} %copy-done), slice={[0:2048], [1024:5248]} | slice | bytes 34603008 | tf_op jit(solution)/shard_map/slice | solution.py:145
  617.2 169.4 %all-reduce.3.cloned.1.call-done = bf16[1024,2048]{1,0:T(8,128)(2,1)} async-done(((bf16[1024,2048]{1,0:T(8,128)(2,1)}), bf16[1024,2048]{1,0:T(8,128)(2,1)}) %all-reduce.3.cloned.1.call-update) | async-done | bytes 4194320 | tf_op jit(solution)/shard_map/psum | solution.py:207
  789.8 11.2 %fusion.19 = f32[512,2,1408]{2,0,1:T(8,128)S(1)} fusion(bf16[2048,3,1408]{0,2,1:T(8,128)(2,1)} %bitcast.195, f32[512,2048]{1,0:T(8,128)S(1)} %get-tuple-element.362, f32[2048]{0:T(1024)S(1)} %copy-done.11, f32[512]{0:T(512)S(1)} %add_rsqrt_fusion.2), kind=kOutput, calls=%fused_computation.37 | convolution fusion | flops 5908725760 | bytes 21506048 | tf_op jit(solution)/shard_map/td,dcf->tcf/dot_general | solution.py:212
  801.1 7.4 fusion.25
  808.5 29.1 %reduce-scatter.2.cloned.1.call-done = bf16[512,512]{1,0:T(8,128)(2,1)} async-done(((bf16[512,2048]{1,0:T(8,128)(2,1)}), bf16[512,512]{1,0:T(8,128)(2,1)}) %reduce-scatter.2.cloned.1.call-update) | async-done | bytes 524304 | tf_op jit(solution)/shard_map/reduce_scatter | solution.py:219
  (267 shorter events, 133.9 us)
Async XLA Ops:
  6.5 3.1 copy-start.5
  43.0 8.6 %copy-start.8 = (s32[8]{0:T(128)S(1)}, s32[8]{0:T(128)}, u32[]{:S(2)}) copy-start(s32[8]{0:T(128)} %param.19) | copy-start | bytes 100
  43.0 8.6 %copy-start.10 = (s32[8]{0:T(128)S(1)}, s32[8]{0:T(128)}, u32[]{:S(2)}) copy-start(s32[8]{0:T(128)} %param.18) | copy-start | bytes 100
  43.0 9.5 %copy-start.9 = (s32[32]{0:T(128)S(1)}, s32[32]{0:T(128)}, u32[]{:S(2)}) copy-start(s32[32]{0:T(128)} %param.20) | copy-start | bytes 388
  43.0 9.7 %copy-start.12 = (u32[128]{0:T(128)S(1)}, u32[128]{0:T(128)}, u32[]{:S(2)}) copy-start(u32[128]{0:T(128)} %constant.161) | copy-start | bytes 1540
  43.0 375.6 %all-to-all-start.1 = ((bf16[16,128,5248]{1,2,0:T(8,128)(2,1)}), bf16[16,128,5248]{1,2,0:T(8,128)(2,1)}, u32[]{:S(2)}, u32[]{:S(2)}) async-start(bf16[16,128,5248]{1,2,0:T(8,128)(2,1)} %stack.3), calls=%async_computation.1 | async-start | bytes 42991616 | tf_op jit(solution)/shard_map/all_to_all | solution.py:141
  51.5 526.9 %all-gather.3.cloned.1.call-start = ((), (), s32[]{:S(2)}) async-start(), calls=%async_computation.5 | async-start | bytes 1114112 | tf_op jit(solution)/shard_map/all_gather | solution.py:26
  406.5 5.2 copy-start.6
  411.6 3.8 copy-start.1
  411.6 3.8 copy-start.7
  429.4 8.8 %copy-start = (bf16[2048,5248]{0,1:T(8,128)(2,1)}, bf16[2048,5248]{0,1:T(8,128)(2,1)S(1)}, u32[]{:S(2)}) copy-start(bf16[2048,5248]{0,1:T(8,128)(2,1)S(1)} %copy_bitcast_fusion.3) | copy-start | bytes 64487428
  429.4 5.3 copy-start.4
  438.2 2.3 copy-start.3
  547.6 239.0 %all-reduce.3.cloned.1.call-start = ((), (), s32[]{:S(2)}) async-start(), calls=%async_computation.3 | async-start | bytes 8388608 | tf_op jit(solution)/shard_map/psum | solution.py:207
  602.2 235.4 %reduce-scatter.2.cloned.1.call-start = ((), (), s32[]{:S(2)}) async-start(), calls=%async_computation.4 | async-start | bytes 2621440 | tf_op jit(solution)/shard_map/reduce_scatter | solution.py:219
  786.6 3.2 copy-start.11
  789.8 11.2 %copy-start.2 = (f32[512,2048]{1,0:T(8,128)}, f32[512,2048]{1,0:T(8,128)S(1)}, u32[]{:S(2)}) copy-start(f32[512,2048]{1,0:T(8,128)S(1)} %get-tuple-element.362) | copy-start | bytes 12582916
Sparse Core Ops, SparseCore 0:
  547.7 30.6 all-gather.2
  602.3 184.2 all-reduce.2
  808.5 29.0 reduce-scatter.1
